TPU v7x, 128 devices: a whole 4x4x4 slice. The times are simulated.
128 devices in a mesh: owner: 64 (over y, x, z), pair: 2 (over core).
Axes of the slice: x: 4, y: 4, z: 4, core: 2. Of those that a mesh axis runs over, the one named last changes fastest.
Arguments:
- incident: float32 [128, 2, 32, 512], P('owner', None, None, 'pair'), may hold values from -6 to 6
- tmat: float32 [128, 2, 512, 512], P('owner', None, 'pair'), may hold values from -0.1875 to 0.1875
- blocks: float32 [1344, 2, 512, 512], P('owner', None, None, 'pair'), may hold values from -0.09375 to 0.09375
- block_rows: int32 [1344], P('owner'), may hold values from 0 to 1
- partners: int32 [1344], replicated, may hold values from 0 to 127, as said below
- live: int32 [64], P('owner'), may hold values from 1 to 21, as said below
- owner_of: int32 [128], replicated, may hold values from 0 to 127, as said below
Outputs:
- scattered: float32 [128, 2, 32, 512], P('owner', None, None, 'pair')
- exciting: float32 [128, 2, 32, 512], P('owner', None, None, 'pair')
Inputs may be any that keep to these rules, and one draw needn't show every extreme that they name: A permutation: particle p's coefficients and T-matrix stand in row owner_of[p]. `partners`: the 21 slots of one owner name distinct particles whose rows lie with owners either less than 8 positions away on either side around the cycle of owners or exactly 32 positions away, never the owner itself, at most 2 with any one other owner; for every owner some other owner holds exactly 2 of them. Slots n with n mod 21 below live[n // 21] are live; some owner has all 21 slots live.
All inputs are finite; a program needn't handle non-finite values.
Results may differ from a plain program's by a relative error of at most 0.0003.
Values sent between devices are 32-bit elements; how exact they have to be, the bound alone decides.
A program may use at most 128 MiB of HBM per device.

v0:
```python
import jax
import jax.numpy as jnp
from jax import lax
from jax.sharding import PartitionSpec as P

ITERS = 2


HIGHEST = lax.Precision.HIGHEST


def complex_rows(matrix, vectors):
    directions = vectors.shape[1]
    stacked = vectors.reshape(2 * directions, vectors.shape[2])
    real_part = jnp.einsum(
        "km,lm->kl", stacked, matrix[0], precision=HIGHEST, preferred_element_type=jnp.float32
    )
    imag_part = jnp.einsum(
        "km,lm->kl", stacked, matrix[1], precision=HIGHEST, preferred_element_type=jnp.float32
    )
    return jnp.stack(
        (
            real_part[:directions] - imag_part[directions:],
            imag_part[:directions] + real_part[directions:],
        )
    )


def complex_cols(matrix, vectors):
    directions = vectors.shape[1]
    stacked = vectors.reshape(2 * directions, vectors.shape[2])
    real_part = jnp.einsum(
        "kl,lm->km", stacked, matrix[0], precision=HIGHEST, preferred_element_type=jnp.float32
    )
    imag_part = jnp.einsum(
        "kl,lm->km", stacked, matrix[1], precision=HIGHEST, preferred_element_type=jnp.float32
    )
    return jnp.stack(
        (
            real_part[:directions] - imag_part[directions:],
            imag_part[:directions] + real_part[directions:],
        )
    )


def gather_field(field_half):
    return lax.all_gather(field_half, "pair", axis=3, tiled=True)


def local(incident, tmat, blocks, block_rows, partners, live, owner_of):
    particles = incident.shape[0]
    directions = incident.shape[2]
    half_width = incident.shape[3]
    block_count = blocks.shape[0]
    my_owner = lax.axis_index("owner")
    particle_ids = jnp.arange(owner_of.shape[0], dtype=jnp.int32)
    every_row = jnp.sum(
        jnp.where(partners[:, None] == particle_ids[None, :], owner_of[None, :], 0), axis=1
    )
    partner_row = lax.dynamic_slice_in_dim(every_row, my_owner * block_count, block_count)
    alive_count = live[0]
    apply_tmat = jax.vmap(complex_rows)

    def coefficients(field_full):
        return (apply_tmat(tmat, field_full), None)

    half_coeff, whole_coeff = coefficients(gather_field(incident))
    exciting = incident
    for iteration in range(ITERS):
        full_coeff = lax.all_gather(half_coeff, "pair", axis=3, tiled=True)
        empty = jnp.zeros((block_count, 2, directions, half_width), jnp.float32)
        shard_rows = lax.all_gather(half_coeff, "owner", axis=0, tiled=True)
        inside = (partner_row >= 0) & (partner_row < shard_rows.shape[0])
        picked_rows = shard_rows[jnp.clip(partner_row, 0, shard_rows.shape[0] - 1)]
        fetched = jnp.where(inside[:, None, None, None], picked_rows, empty)

        def apply_block(block_index, totals):
            near_acc, given_back = totals
            one_block = lax.dynamic_index_in_dim(blocks, block_index, 0, keepdims=False)
            holder_row = block_rows[block_index]
            forward = complex_rows(one_block, fetched[block_index])
            near_acc = near_acc.at[holder_row].add(forward)
            backward = complex_cols(one_block, full_coeff[holder_row])
            given_back = given_back.at[block_index].set(backward)
            return (near_acc, given_back)

        start_near = jnp.zeros((particles, 2, directions, full_coeff.shape[3]), jnp.float32)
        start_back = jnp.zeros((block_count, 2, directions, half_width), jnp.float32)
        near_acc, given_back = lax.fori_loop(0, alive_count, apply_block, (start_near, start_back))
        near_field = lax.psum_scatter(near_acc, "pair", scatter_dimension=3, tiled=True)
        stacked_rows = given_back.reshape(block_count, -1)
        row_ids = jnp.arange(particles * lax.axis_size("owner"), dtype=jnp.int32)
        chosen = (row_ids[:, None] == partner_row[None, :]).astype(jnp.float32)
        summed = jnp.dot(
            chosen, stacked_rows, precision=HIGHEST, preferred_element_type=jnp.float32
        )
        returned = lax.psum_scatter(
            summed.reshape(particles * lax.axis_size("owner"), 2, directions, half_width),
            "owner",
            scatter_dimension=0,
            tiled=True,
        )
        exciting = incident + near_field + returned
        half_coeff, whole_coeff = coefficients(gather_field(exciting))
    return (half_coeff, exciting)


def solution(mesh):
    in_specs = (
        P("owner", None, None, "pair"),
        P("owner", None, "pair", None),
        P("owner", None, None, "pair"),
        P("owner"),
        P(),
        P("owner"),
        P(),
    )
    out_specs = (P("owner", None, None, "pair"), P("owner", None, None, "pair"))
    return jax.shard_map(local, mesh=mesh, in_specs=in_specs, out_specs=out_specs, check_vma=False)
```

profile of v0, /device:TPU:1, one launch (start us, length us, event | category | flops | bytes accessed | tf_op | source)
XLA Modules:
  0.0 1576.0 jit_solution(6190756898155032191)
XLA Ops:
  18.7 78.3 %all-gather.3.cloned.1.call-done = f32[128,2,32,256]{3,2,0,1:T(8,128)} async-done(((f32[2,2,32,256]{3,2,0,1:T(8,128)}), f32[128,2,32,256]{3,2,0,1:T(8,128)}) %all-gather.3.cloned.1.call-update) | async-done | bytes 8388624 | tf_op jit(solution)/shard_map/all_gather | solution.py:72
  96.9 4.0 gather_fusion
  101.7 208.7 %while.28 = (s32[]{:T(128)}, f32[2,2,32,512]{3,2,1,0:T(8,128)S(1)}, f32[21,2,32,256]{3,2,1,0:T(8,128)S(1)}, s32[]{:T(128)}, s32[21]{0:T(128)S(1)}, /*index=5*/f3...) while((s32[]{:T(128)}, f32[2,2,32,512]{3,2,1,0:T(8,128)S(1)}, ...), condition=%wide.region_4.5_spmd, body=%wide.region_1.4_spmd.sunk | while | flops 402833472 | bytes 4458809 | solution.py:89
  310.3 13.7 copy.92
  324.1 13.1 reshape.209
  337.5 3.7 fusion.32
  341.2 8.1 copy.81
  349.3 46.7 %reduce-scatter.13.cloned.1.call-done = f32[256,128]{1,0:T(8,128)} async-done(((f32[512,128]{1,0:T(8,128)}), f32[256,128]{1,0:T(8,128)}) %reduce-scatter.13.cloned.1.call-update) | async-done | bytes 131088
  396.0 10.4 reshape.210
  406.5 6.5 copy.79
  413.0 310.1 %reduce-scatter.9.cloned.1.call-done = f32[2,2,32,256]{3,2,1,0:T(8,128)} async-done(((f32[128,2,32,256]{3,2,1,0:T(8,128)}), f32[2,2,32,256]{3,2,1,0:T(8,128)}) %reduce-scatter.9.cloned.1.call-update) | async-done | bytes 131088 | tf_op jit(solution)/shard_map/reduce_scatter | solution.py:97
  724.1 63.5 %all_gather.24 = f32[2,2,32,512]{3,2,1,0:T(8,128)S(1)} all-gather(f32[2,2,32,256]{3,2,1,0:T(8,128)S(1)} %add_add_fusion), channel_id=1, replica_groups=mesh['owner'=64,'pair'=2] {'pair'}, dimensions={3}, use_global_device_ids=true | all-gather | bytes 393216 | tf_op jit(solution)/shard_map/all_gather | solution.py:47
  792.7 71.1 %all-gather.5.cloned.1.call-done = f32[128,2,32,256]{3,2,0,1:T(8,128)} async-done(((f32[2,2,32,256]{3,2,0,1:T(8,128)}), f32[128,2,32,256]{3,2,0,1:T(8,128)}) %all-gather.5.cloned.1.call-update) | async-done | bytes 8388624 | tf_op jit(solution)/shard_map/all_gather | solution.py:72
  863.8 5.2 gather_fusion.1
  872.9 225.5 %while.29 = (s32[]{:T(128)}, f32[2,2,32,512]{3,2,1,0:T(8,128)S(1)}, f32[21,2,32,256]{3,2,1,0:T(8,128)}, s32[]{:T(128)}, s32[21]{0:T(128)S(1)}, /*index=5*/f32[21...) while((s32[]{:T(128)}, f32[2,2,32,512]{3,2,1,0:T(8,128)S(1)}, ...), condition=%wide.region_10.11_spmd, body=%wide.region_7.10_spmd.sunk | while | flops 402833472 | bytes 4459828 | solution.py:89
  1098.4 13.7 copy.94
  1112.2 13.1 reshape.211
  1125.4 5.0 fusion.30
  1130.4 8.1 copy.86
  1138.5 49.6 %reduce-scatter.15.cloned.1.call-done = f32[256,128]{1,0:T(8,128)} async-done(((f32[512,128]{1,0:T(8,128)}), f32[256,128]{1,0:T(8,128)}) %reduce-scatter.15.cloned.1.call-update) | async-done | bytes 131088
  1188.1 10.4 reshape.212
  1198.6 6.4 copy.95
  1204.9 311.5 %reduce-scatter.11.cloned.1.call-done = f32[2,2,32,256]{3,2,1,0:T(8,128)} async-done(((f32[128,2,32,256]{3,2,1,0:T(8,128)}), f32[2,2,32,256]{3,2,1,0:T(8,128)}) %reduce-scatter.11.cloned.1.call-update) | async-done | bytes 131088 | tf_op jit(solution)/shard_map/reduce_scatter | solution.py:97
  1517.5 47.7 %all_gather.27 = f32[2,2,32,512]{3,0,2,1:T(2,128)S(1)} all-gather(f32[2,2,32,256]{3,0,2,1:T(2,128)S(1)} %copy_add_fusion), channel_id=1, replica_groups=mesh['owner'=64,'pair'=2] {'pair'}, dimensions={3}, use_global_device_ids=true | all-gather | bytes 393216 | tf_op jit(solution)/shard_map/all_gather | solution.py:47
  (464 shorter events, 376.1 us)
Async XLA Ops:
  7.2 89.8 %all-gather.3.cloned.1.call-start = ((), (), s32[]{:S(2)}) async-start(), calls=%async_computation.4 | async-start | bytes 8519680 | tf_op jit(solution)/shard_map/all_gather | solution.py:72
  10.4 7.7 copy-start.4
  10.4 7.7 copy-start.5
  15.8 380.2 %reduce-scatter.13.cloned.1.call-start = ((), (), s32[]{:S(2)}) async-start(), calls=%async_computation.8 | async-start | bytes 393216
  101.0 0.7 copy-start.2
  101.0 0.7 copy-start.3
  101.0 0.7 copy-start.6
  337.2 385.9 %reduce-scatter.9.cloned.1.call-start = ((), (), s32[]{:S(2)}) async-start(), calls=%async_computation.5 | async-start | bytes 8519680 | tf_op jit(solution)/shard_map/reduce_scatter | solution.py:97
  349.3 514.5 %all-gather.5.cloned.1.call-start = ((), (), s32[]{:S(2)}) async-start(), calls=%async_computation.6 | async-start | bytes 8519680 | tf_op jit(solution)/shard_map/all_gather | solution.py:72
  406.5 316.7 %copy-start.1 = (f32[2,2,32,256]{3,2,1,0:T(8,128)S(1)}, f32[2,2,32,256]{3,2,1,0:T(8,128)}, u32[]{:S(2)}) copy-start(f32[2,2,32,256]{3,2,1,0:T(8,128)} %param.19) | copy-start | bytes 393220
  406.5 381.1 %copy-start = (f32[2,2,256,512]{3,2,1,0:T(8,128)S(1)}, f32[2,2,256,512]{3,2,1,0:T(8,128)}, u32[]{:S(2)}) copy-start(f32[2,2,256,512]{3,2,1,0:T(8,128)} %param.20) | copy-start | bytes 6291460
  790.5 397.6 %reduce-scatter.15.cloned.1.call-start = ((), (), s32[]{:S(2)}) async-start(), calls=%async_computation.9 | async-start | bytes 393216
  1125.3 391.1 %reduce-scatter.11.cloned.1.call-start = ((), (), s32[]{:S(2)}) async-start(), calls=%async_computation.7 | async-start | bytes 8519680 | tf_op jit(solution)/shard_map/reduce_scatter | solution.py:97
Sparse Core Ops, SparseCore 0:
  16.0 80.9 all-gather.2
  337.3 58.6 reduce-scatter.12
  398.4 324.6 reduce-scatter.8
  790.6 73.1 all-gather.4
  1125.4 62.6 reduce-scatter.14
  1190.4 325.9 reduce-scatter.10
where the time goes:
time: 1580 us
  waiting for transfers between devices  867 us (55%)
  matrix products  227 us (14%)
  local copies, waits for them, and re-layouts  137 us (9%)
  other arithmetic  125 us (8%)
  blocking collectives  119 us (8%)
  loops' own time  85.5 us (5%)
    reduce_scatter x2, waiting for transfers between devices, local(): lax.psum_scatter(summed.reshape(particles * lax.axis_size('owner'), 2, di...  622 us
    all_gather x2, waiting for transfers between devices, local(): shard_rows = lax.all_gather(half_coeff, 'owner', axis=0, tiled=True)  149 us
    all_gather x3, blocking collectives, gather_field(): return lax.all_gather(field_half, 'pair', axis=3, tiled=True)  114 us
    unnamed x8, waiting for transfers between devices  96.4 us
    another operation x2, loops' own time, local(): lax.fori_loop(0, alive_count, apply_block, (start_near, start_back))  85.5 us
    unnamed x23, local copies, waits for them, and re-layouts  82.6 us
    dot_general x37, matrix products, complex_rows(): jnp.einsum('km,lm->kl', stacked, matrix[1], precision=HIGHEST, preferred_...  60.7 us
    dot_general x37, matrix products, complex_rows(): jnp.einsum('km,lm->kl', stacked, matrix[0], precision=HIGHEST, preferred_...  60.6 us
  transfers between devices with their start and end apart: 6, of which 6 were waited for; matrix products, arithmetic and copies ran while one was open for 4% of the time, Pallas kernels for 0%

commit v1 on v0

v1 whole, which is shorter than its diff:
```python
import functools

import jax
import jax.numpy as jnp
from jax import lax
from jax.experimental import pallas as pl
from jax.experimental.pallas import tpu as pltpu
from jax.sharding import PartitionSpec as P

ITERS = 2
SLOTS = 21
STAGES = 4
ROWS = 64
HALF = 256
MESH = pl.DeviceIdType.MESH
F32 = jnp.float32
BF16 = jnp.bfloat16


def split(x):
    hi = x.astype(BF16)
    lo = (x - hi.astype(F32)).astype(BF16)
    return hi, lo


def turned(v):
    return jnp.concatenate([-v[ROWS // 2 :], v[: ROWS // 2]], axis=0)


def dot_nn(a, b):
    return lax.dot_general(a, b, (((1,), (0,)), ((), ())), preferred_element_type=F32)


def dot_nt(a, b):
    return lax.dot_general(a, b, (((1,), (1,)), ((), ())), preferred_element_type=F32)


def stacked_parts(v):
    hi, lo = split(v)
    return jnp.concatenate([hi, lo], axis=0)


def kernel(
    meta, incident, tmat, blocks, out_s, out_e,
    field_a, field_b, transit, give, result, from_x, line_sum, line_in, from_z, cross_sum, cross_in,
    pair_e, pair_h, pair_n, near, m_hi, m_lo, stage, t_hi, t_lo, wide,
    f_send, f_recv, g_send, g_recv, p_send, p_recv, stage_sem,
):
    me = lax.axis_index("owner")
    core = lax.axis_index("pair")
    z = lax.rem(me, 4)
    group = lax.div(me, 4)

    def along_z(j):
        return group * 4 + lax.rem(z + j, 4)

    def along_g(dg):
        return lax.rem(group + dg + 16, 16) * 4 + z

    def to_owner(owner):
        return {"owner": owner}

    other_core = {"pair": 1 - core}

    def remote(src, dst, ssem, rsem, dev):
        return pltpu.make_async_remote_copy(
            src_ref=src, dst_ref=dst, send_sem=ssem, recv_sem=rsem,
            device_id=dev, device_id_type=MESH,
        )

    def fetch_block(n):
        return pltpu.make_async_copy(
            blocks.at[n], stage.at[lax.rem(n, STAGES)], stage_sem.at[lax.rem(n, STAGES)]
        )

    for n in range(STAGES):
        pltpu.make_async_copy(blocks.at[n], stage.at[n], stage_sem.at[n]).start()

    barrier = pltpu.get_barrier_semaphore()
    partners = [along_z(j) for j in (1, 2, 3)] + [along_g(d) for d in (1, -1, 2, -2, 8)]
    for owner in partners:
        pl.semaphore_signal(barrier, inc=1, device_id=to_owner(owner), device_id_type=MESH)
    pl.semaphore_signal(barrier, inc=1, device_id=other_core, device_id_type=MESH)
    pl.semaphore_wait(barrier, 9)

    fields = (field_a, field_b)
    sends = []

    pair0 = remote(incident, pair_e.at[0], p_send.at[0], p_recv.at[0], other_core)
    pair0.start()
    sends.append(pair0)

    for p in range(2):
        for c in range(2):
            hi, lo = split(tmat[p, c])
            t_hi[p, c] = hi
            t_lo[p, c] = lo

    def whole(mine, theirs):
        return jnp.concatenate(
            [jnp.where(core == 0, mine, theirs), jnp.where(core == 0, theirs, mine)], axis=1
        )

    def apply_t(p, v):
        a = stacked_parts(v)
        b = stacked_parts(turned(v))
        big = dot_nt(a, t_hi[p, 0]) + dot_nt(b, t_hi[p, 1])
        small = dot_nt(a[:ROWS], t_lo[p, 0]) + dot_nt(b[:ROWS], t_lo[p, 1])
        return big[:ROWS] + big[ROWS:] + small

    pair0.wait_recv()
    for p in range(2):
        fields[0][16 * p] = apply_t(p, whole(incident[p], pair_e[0, p]))

    for it in range(ITERS):
        ns = [0]
        field = fields[it]

        def send_field(src, dst, recv_index, owner, it=it, ns=ns):
            k = ns[0]
            ns[0] += 1
            c = remote(src, dst, f_send.at[it, k], f_recv.at[it, recv_index], to_owner(owner))
            c.start()
            sends.append(c)

        def got_field(index, it=it, field=field):
            ref = field.at[index] if index < 32 else transit.at[it, index - 32]
            pltpu.make_async_copy(ref, ref, f_recv.at[it, index]).wait()

        def q0(kind, j):
            return kind * 4 + j

        def q1(kind, j):
            return 16 + j * 4 + kind

        halves = []
        for p in range(2):
            c = remote(
                field.at[16 * p], pair_h.at[it, p], p_send.at[3 + it * 2 + p],
                p_recv.at[3 + it * 2 + p], other_core,
            )
            c.start()
            sends.append(c)
            halves.append(c)
        own0 = field.at[0]
        own1 = field.at[16]
        for j in (1, 3, 2):
            send_field(own0, field.at[q0(0, 4 - j)], q0(0, 4 - j), along_z(j))
        for dg, kind in ((1, 2), (-1, 1)):
            send_field(own1, field.at[q1(kind, 0)], q1(kind, 0), along_g(dg))
        for dg, t in ((2, 1), (-2, 0)):
            send_field(own1, transit.at[it, t], 32 + t, along_g(dg))
        for dg, kind in ((1, 2), (-1, 1)):
            send_field(own0, field.at[q0(kind, 0)], q0(kind, 0), along_g(dg))
        for j in (1, 3, 2):
            send_field(own1, field.at[q1(0, 4 - j)], q1(0, 4 - j), along_z(j))
        send_field(own0, field.at[q0(3, 0)], q0(3, 0), along_g(8))
        send_field(own1, field.at[q1(3, 0)], q1(3, 0), along_g(8))

        for p in range(2):
            halves[p].wait_recv()
            v = whole(field[16 * p], pair_h[it, p])
            wide[p, :, : 2 * HALF] = stacked_parts(v)
            wide[p, :, 2 * HALF :] = stacked_parts(turned(v))

        def load_block(n):
            fetch_block(n).wait()
            for c in range(2):
                hi, lo = split(stage[lax.rem(n, STAGES), c])
                m_hi[n, c * 512 : (c + 1) * 512] = hi
                m_lo[n, c * 512 : (c + 1) * 512] = lo

            @pl.when(n + STAGES < SLOTS)
            def _():
                fetch_block(n + STAGES).start()

        def backward(n, carry, it=it):
            if it == 0:
                load_block(n)
            left = wide[meta[SLOTS + n]]
            big = dot_nn(left, m_hi[n])
            small = dot_nn(left[:ROWS], m_lo[n])
            result[n] = big[:ROWS] + big[ROWS:] + small
            return carry

        lax.fori_loop(0, 10, backward, 0)

        for j in (1, 3, 2):
            got_field(q0(0, j))
            line = field.at[q0(0, j)]
            for dg, kind in ((1, 2), (-1, 1)):
                send_field(line, field.at[q0(kind, j)], q0(kind, j), along_g(dg))
            above = lax.rem(z + j, 4) > z
            send_field(
                line, field.at[q0(3, j)], q0(3, j),
                jnp.where(above, along_g(2), along_g(-2)),
            )
        for kind in (1, 2):
            got_field(q1(kind, 0))
            for j in (1, 3, 2):
                send_field(
                    field.at[q1(kind, 0)], field.at[q1(kind, 4 - j)],
                    q1(kind, 4 - j), along_z(j),
                )
        got_field(32)
        got_field(33)
        for j in (1, 3, 2):
            above = lax.rem(z + j, 4) > z
            send_field(
                transit.at[it, jnp.where(above, 0, 1)], field.at[q1(3, 4 - j)],
                q1(3, 4 - j), along_z(j),
            )

        lax.fori_loop(10, SLOTS, backward, 0)

        def fill(k, carry, it=it):
            flag = meta[3 * SLOTS + 33 + k].astype(F32)
            give[it, k] = result[meta[3 * SLOTS + 1 + k]] * flag
            return carry

        lax.fori_loop(1, 32, fill, 0)

        ng = [0]

        def send_give(src, dst, recv_index, owner, it=it, ng=ng):
            k = ng[0]
            ng[0] += 1
            c = remote(src, dst, g_send.at[it, k], g_recv.at[it, recv_index], to_owner(owner))
            c.start()
            sends.append(c)

        def got_give(ref, index, it=it):
            pltpu.make_async_copy(ref, ref, g_recv.at[it, index]).wait()

        send_give(give.at[it, 4:8], from_x.at[it, 1], 1, along_g(1))
        send_give(give.at[it, 8:12], from_x.at[it, 0], 0, along_g(-1))
        for j in (1, 3, 2):
            send_give(give.at[it, pl.ds(16 + 4 * j, 4)], from_z.at[it, 4 - j], 6 + 4 - j, along_z(j))
        for j in (1, 2, 3):
            below = lax.rem(z + j, 4) < z
            send_give(
                give.at[it, q0(3, j)], from_x.at[it, 2, j], 2 + j,
                jnp.where(below, along_g(2), along_g(-2)),
            )
        send_give(give.at[it, q0(3, 0)], from_x.at[it, 2, 0], 2, along_g(8))
        send_give(give.at[it, q1(3, 0)], from_z.at[it, 0, 3], 6, along_g(8))

        for kind in range(4):
            for j in range(4):
                if kind == 0 and j == 0:
                    continue
                if not (kind == 0):
                    got_field(q0(kind, j))
                if not (j == 0 and kind in (1, 2)):
                    got_field(q1(kind, j))

        for h in range(2):
            for p in range(2):
                near[it, h, p] = jnp.zeros((ROWS, HALF), F32)

        def forward(n, carry, it=it, field=field):
            v = field[meta[n]]
            a = stacked_parts(v)
            b = stacked_parts(turned(v))
            big = dot_nt(a, m_hi[n, :512]) + dot_nt(b, m_hi[n, 512:])
            small = dot_nt(a[:ROWS], m_lo[n, :512]) + dot_nt(b[:ROWS], m_lo[n, 512:])
            out = big[:ROWS] + big[ROWS:] + small
            alive = meta[2 * SLOTS + n].astype(F32)
            second = alive * meta[SLOTS + n].astype(F32)
            first = alive - second
            for h in range(2):
                part = out[:, h * HALF : (h + 1) * HALF]
                near[it, h, 0] += part * first
                near[it, h, 1] += part * second
            return carry

        lax.fori_loop(0, 10, forward, 0)

        for k in range(2):
            got_give(from_x.at[it, k], k)
        for j in range(1, 4):
            got_give(from_x.at[it, 2, j], 2 + j)
            line_sum[it, j] = (
                give[it, q0(0, j)] + from_x[it, 0, j] + from_x[it, 1, j] + from_x[it, 2, j]
            )
        for j in (1, 3, 2):
            send_give(line_sum.at[it, j], line_in.at[it, 4 - j], 10 + 4 - j, along_z(j))
        for j in range(1, 4):
            got_give(from_z.at[it, j], 6 + j)
        for k, kind in ((0, 1), (1, 2)):
            cross_sum[it, k] = (
                give[it, q1(kind, 0)]
                + from_z[it, 1, kind] + from_z[it, 2, kind] + from_z[it, 3, kind]
            )
        up = jnp.zeros((ROWS, HALF), F32)
        down = jnp.zeros((ROWS, HALF), F32)
        for j in range(1, 4):
            term = from_z[it, j, 3]
            above = (lax.rem(z + j, 4) > z).astype(F32)
            up += term * above
            down += term * (1.0 - above)
        cross_sum[it, 2] = up
        cross_sum[it, 3] = down
        for k, dg in ((0, 1), (1, -1), (2, 2), (3, -2)):
            send_give(cross_sum.at[it, k], cross_in.at[it, k], 14 + k, along_g(dg))

        lax.fori_loop(10, SLOTS, forward, 0)

        c = remote(
            near.at[it, 1 - core], pair_n.at[it], p_send.at[7 + it], p_recv.at[7 + it], other_core
        )
        c.start()
        sends.append(c)

        got_give(from_x.at[it, 2, 0], 2)
        got_give(from_z.at[it, 0, 3], 6)
        for j in range(1, 4):
            got_give(line_in.at[it, j], 10 + j)
        for k in range(4):
            got_give(cross_in.at[it, k], 14 + k)
        c.wait_recv()
        returned0 = (
            from_x[it, 0, 0] + from_x[it, 1, 0] + from_x[it, 2, 0]
            + line_in[it, 1] + line_in[it, 2] + line_in[it, 3]
        )
        returned1 = (
            from_z[it, 1, 0] + from_z[it, 2, 0] + from_z[it, 3, 0] + from_z[it, 0, 3]
            + cross_in[it, 0] + cross_in[it, 1] + cross_in[it, 2] + cross_in[it, 3]
        )
        out_e[0] = incident[0] + near[it, core, 0] + pair_n[it, 0] + returned0
        out_e[1] = incident[1] + near[it, core, 1] + pair_n[it, 1] + returned1
        swap = remote(
            out_e, pair_e.at[1 + it], p_send.at[1 + it], p_recv.at[1 + it], other_core
        )
        swap.start()
        swap.wait()
        for p in range(2):
            after = apply_t(p, whole(out_e[p], pair_e[1 + it, p]))
            if it + 1 < ITERS:
                fields[it + 1][16 * p] = after
            else:
                out_s[p] = after

    for c in sends:
        c.wait_send()


def tables(block_rows, partners, live, owner_of):
    me = lax.axis_index("owner")
    z = me % 4
    group = me // 4
    mine = lax.dynamic_slice(partners, (me * SLOTS,), (SLOTS,))
    ids = jnp.arange(owner_of.shape[0], dtype=jnp.int32)
    rows = jnp.sum(jnp.where(mine[:, None] == ids[None, :], owner_of[None, :], 0), axis=1)
    owner = rows // 2
    j = (owner % 4 - z) % 4
    dg = (owner // 4 - group) % 16
    kind = jnp.where(dg == 0, 0, jnp.where(dg == 1, 1, jnp.where(dg == 15, 2, 3)))
    where_ = jnp.where(rows % 2 == 0, kind * 4 + j, 16 + j * 4 + kind)
    slots = jnp.arange(SLOTS, dtype=jnp.int32)
    alive = (slots < live[0]).astype(jnp.int32)
    hit = (where_[None, :] == jnp.arange(32, dtype=jnp.int32)[:, None]) & (alive[None, :] > 0)
    slot_of = jnp.sum(jnp.where(hit, slots[None, :], 0), axis=1)
    found = jnp.sum(hit.astype(jnp.int32), axis=1)
    pad = jnp.zeros((1,), jnp.int32)
    return jnp.concatenate([where_, block_rows, alive, pad, slot_of, found]).astype(jnp.int32)


def local(incident, tmat, blocks, block_rows, partners, live, owner_of):
    meta = tables(block_rows, partners, live, owner_of)
    inc = incident.reshape(2, ROWS, HALF)
    vm = lambda shape, dt=F32: pltpu.VMEM(shape, dt)
    h = (ROWS, HALF)
    sem = pltpu.SemaphoreType.DMA
    shape = jax.ShapeDtypeStruct((2, ROWS, HALF), F32)
    scattered, exciting = pl.pallas_call(
        kernel,
        out_shape=(shape, shape),
        in_specs=[
            pl.BlockSpec(memory_space=pltpu.SMEM),
            pl.BlockSpec(memory_space=pltpu.VMEM),
            pl.BlockSpec(memory_space=pltpu.VMEM),
            pl.BlockSpec(memory_space=pl.ANY),
        ],
        out_specs=(pl.BlockSpec(memory_space=pltpu.VMEM),) * 2,
        scratch_shapes=[
            vm((32,) + h), vm((32,) + h), vm((2, 2) + h), vm((2, 32) + h), vm((SLOTS,) + h),
            vm((2, 3, 4) + h), vm((2, 4) + h), vm((2, 4) + h), vm((2, 4, 4) + h),
            vm((2, 4) + h), vm((2, 4) + h),
            vm((3, 2) + h), vm((2, 2) + h), vm((2, 2) + h), vm((2, 2, 2) + h),
            vm((SLOTS, 1024, HALF), BF16), vm((SLOTS, 1024, HALF), BF16),
            vm((STAGES, 2, 512, HALF)),
            vm((2, 2, HALF, 512), BF16), vm((2, 2, HALF, 512), BF16),
            vm((2, 2 * ROWS, 1024), BF16),
            sem((2, 32)), sem((2, 34)), sem((2, 17)), sem((2, 18)), sem((9,)), sem((9,)),
            sem((STAGES,)),
        ],
        compiler_params=pltpu.CompilerParams(
            collective_id=0, has_side_effects=True, vmem_limit_bytes=60 * 1024 * 1024
        ),
        name="scatter_steps",
    )(meta, inc, tmat, blocks)
    full = (2, 2, ROWS // 2, HALF)
    return scattered.reshape(full), exciting.reshape(full)


def solution(mesh):
    in_specs = (
        P("owner", None, None, "pair"),
        P("owner", None, "pair", None),
        P("owner", None, None, "pair"),
        P("owner"),
        P(),
        P("owner"),
        P(),
    )
    out_specs = (P("owner", None, None, "pair"), P("owner", None, None, "pair"))
    return jax.shard_map(local, mesh=mesh, in_specs=in_specs, out_specs=out_specs, check_vma=False)
```

time: 1580 us -> 99.5 us (0.06)
  waiting for transfers between devices: 867 us -> 0 us
  matrix products: 227 us -> 0 us
  local copies, waits for them, and re-layouts: 137 us -> 5.16 us
  other arithmetic: 125 us -> 0.97 us
  blocking collectives: 119 us -> 0 us
  Pallas kernels: 0 us -> 91.8 us
  loops' own time: 85.5 us -> 0 us
    reduce_scatter x2 -> x0, waiting for transfers between devices: 622 us -> none  [local(): lax.psum_scatter(summed.reshape(particles * lax.axis_size('owner'), 2, di...]
    dot_general x144 -> x0, matrix products: 227 us -> none  [the longest x37 60.7 us: complex_rows(): jnp.einsum('km,lm->kl', stacked, matrix[1], precision=HIGHEST, preferred_...]
    all_gather x2 -> x0, waiting for transfers between devices: 149 us -> none  [local(): shard_rows = lax.all_gather(half_coeff, 'owner', axis=0, tiled=True)]
    all_gather x5 -> x0, blocking collectives: 119 us -> none  [the longest x3 114 us: gather_field(): return lax.all_gather(field_half, 'pair', axis=3, tiled=True)]
    unnamed x8 -> x0, waiting for transfers between devices: 96.4 us -> none
    pallas_call x0 -> x1, Pallas kernels: none -> 91.8 us  [local(): pl.pallas_call(kernel, out_shape=(shape, shape), in_specs=[pl.BlockSpec(m...]
    another operation x2 -> x0, loops' own time: 85.5 us -> none  [local(): lax.fori_loop(0, alive_count, apply_block, (start_near, start_back))]
    unnamed x23 -> x2, local copies, waits for them, and re-layouts: 82.6 us -> 3.14 us
  transfers between devices with their start and end apart: 6 -> 0, of which waited for: 6 -> 0; matrix products, arithmetic and copies ran while one was open for 4% -> 0% of each run, Pallas kernels for 0% -> 0%
where the time goes in v1:
time: 99.5 us; the launch traced here: 99.2 us
  Pallas kernels  91.8 us (92%)
  local copies, waits for them, and re-layouts  5.16 us (5%)
  between operations  1.32 us (1%)
    pallas_call x1, Pallas kernels, local(): pl.pallas_call(kernel, out_shape=(shape, shape), in_specs=[pl.BlockSpec(m...  91.8 us
    unnamed x2, local copies, waits for them, and re-layouts  3.14 us

profile of v1, /device:TPU:1, one launch (start us, length us, event | category | flops | bytes accessed | tf_op | source)
XLA Modules:
  0.0 99.2 jit_solution(6309862911605737094)
XLA Ops:
  1.3 0.8 dynamic_slice.3
  2.1 0.8 select_reduce_fusion.1
  3.0 0.1 convert_reduce_fusion
  3.1 1.2 %concatenate.3.meta = s32[128]{0:T(128)} concatenate(s32[21]{0:T(128)S(1)} %compare_select_fusion.7, s32[21]{0:T(128)} %param.10, s32[21]{0:T(128)S(1)} %get-tuple-element.8, s32[1]{0:T(128)} %constant.104.clone.1, s32[32]{0:T(128)S(1)} %get-tuple-element.7, s32[32]{0:T(128)S(1)} %get-tuple-element.6), dimensions={0} | concatenate | bytes 1024 | tf_op jit(solution)/shard_map/concatenate | solution.py:366
  4.3 91.8 %scatter_steps.1 = (f32[2,64,256]{2,1,0:T(8,128)}, f32[2,64,256]{2,1,0:T(8,128)}) custom-call(s32[128]{0:T(128)} %concatenate.3.meta, f32[2,64,256]{2,1,0:T(8,128)} %bitcast.5, f32[2,2,256,512]{3,2,1,0:T(8,128)} %tmat.1, f32[21,2,512,256]{3,2,1,0:T(8,128)} %blocks.1), custom_call_target="tpu_custom_call" | custom-call | tf_op jit(solution)/shard_map/scatter_steps/pallas_call | solution.py:376
  96.1 1.6 %copy.12 = f32[2,2,32,256]{3,2,1,0:T(8,128)} copy(f32[2,2,32,256]{3,2,1,0:T(8,128)} %bitcast.7) | data formatting | bytes 262144
  97.7 1.6 %copy.13 = f32[2,2,32,256]{3,2,1,0:T(8,128)} copy(f32[2,2,32,256]{3,2,1,0:T(8,128)} %bitcast.6) | data formatting | bytes 262144
  (2 shorter events, 0.0 us)

commit v2 on v1

v2 whole, which is shorter than its diff:
```python
import functools

import jax
import jax.numpy as jnp
from jax import lax
from jax.experimental import pallas as pl
from jax.experimental.pallas import tpu as pltpu
from jax.sharding import PartitionSpec as P

ITERS = 2
SLOTS = 21
STAGES = 4
ROWS = 64
HALF = 256
MESH = pl.DeviceIdType.MESH
F32 = jnp.float32
BF16 = jnp.bfloat16


def split(x):
    hi = x.astype(BF16)
    lo = (x - hi.astype(F32)).astype(BF16)
    return hi, lo


def turned(v):
    return jnp.concatenate([-v[ROWS // 2 :], v[: ROWS // 2]], axis=0)


def dot_nn(a, b):
    return lax.dot_general(a, b, (((1,), (0,)), ((), ())), preferred_element_type=F32)


def dot_nt(a, b):
    return lax.dot_general(a, b, (((1,), (1,)), ((), ())), preferred_element_type=F32)


def stacked_parts(v):
    hi, lo = split(v)
    return jnp.concatenate([hi, lo], axis=0)


def kernel(
    partners_ref, owner_ref, rows_ref, live_ref, incident, tmat, blocks, out_s, out_e,
    field_a, field_b, transit, through_f, through_g, give, result, from_x, line_sum, line_in, from_z, cross_sum, cross_in,
    pair_e, pair_h, pair_n, near, m_hi, m_lo, stage, t_raw, t_hi, t_lo, wide,
    place, key, slot_of, found, f_send, f_recv, g_send, g_recv, p_send, p_recv, stage_sem, t_sem,
):
    me = lax.axis_index("owner")
    core = lax.axis_index("pair")
    z = lax.rem(me, 4)
    group = lax.div(me, 4)

    def along_z(j):
        return group * 4 + lax.rem(z + j, 4)

    def along_g(dg):
        return lax.rem(group + dg + 16, 16) * 4 + z

    x = lax.rem(group, 4)
    y = lax.div(group, 4)
    y_way = jnp.where(x < 2, 3, 1)
    even = lax.rem(z, 2) == 0

    def along_y(dy):
        return (lax.rem(y + dy, 4) * 4 + x) * 4 + z

    def to_owner(owner):
        return {"owner": owner}

    other_core = {"pair": 1 - core}

    def remote(src, dst, ssem, rsem, dev):
        return pltpu.make_async_remote_copy(
            src_ref=src, dst_ref=dst, send_sem=ssem, recv_sem=rsem,
            device_id=dev, device_id_type=MESH,
        )

    def fetch_block(n):
        return pltpu.make_async_copy(
            blocks.at[n], stage.at[lax.rem(n, STAGES)], stage_sem.at[lax.rem(n, STAGES)]
        )

    barrier = pltpu.get_barrier_semaphore()
    partners = [along_z(j) for j in (1, 2, 3)] + [along_g(d) for d in (1, -1, 2, -2)]
    partners += [along_y(1), along_y(3)]
    pl.semaphore_signal(barrier, inc=1, device_id=other_core, device_id_type=MESH)
    for owner in partners:
        pl.semaphore_signal(barrier, inc=1, device_id=to_owner(owner), device_id_type=MESH)

    t_copy = pltpu.make_async_copy(tmat, t_raw, t_sem.at[0])
    t_copy.start()
    for n in range(STAGES):
        pltpu.make_async_copy(blocks.at[n], stage.at[n], stage_sem.at[n]).start()

    def find(n, carry):
        row = owner_ref[partners_ref[me * SLOTS + n]]
        owner = lax.div(row, 2)
        j = lax.rem(lax.rem(owner, 4) - z + 4, 4)
        dg = lax.rem(lax.div(owner, 4) - group + 16, 16)
        kind = jnp.where(dg == 0, 0, jnp.where(dg == 1, 1, jnp.where(dg == 15, 2, 3)))
        which = lax.rem(row, 2)
        place[n] = (kind * 4 + j) * 2 + which
        at = jnp.where(which == 0, kind * 4 + j, 16 + j * 4 + kind)
        key[n] = jnp.where(n < live_ref[0], at, -1)
        return carry

    def invert(k, carry):
        slot = jnp.int32(0)
        flag = jnp.int32(0)
        for n in range(SLOTS):
            hit = key[n] == k
            slot = jnp.where(hit, n, slot)
            flag = jnp.where(hit, 1, flag)
        slot_of[k] = slot
        found[k] = flag
        return carry

    t_copy.wait()
    for p in range(2):
        for c in range(2):
            hi, lo = split(t_raw[p, c])
            t_hi[p, c] = hi
            t_lo[p, c] = lo

    pl.semaphore_wait(barrier, 10)

    fields = (field_a, field_b)
    sends = []

    pair0 = remote(incident, pair_e.at[0], p_send.at[0], p_recv.at[0], other_core)
    pair0.start()
    sends.append(pair0)

    def whole(mine, theirs):
        return jnp.concatenate(
            [jnp.where(core == 0, mine, theirs), jnp.where(core == 0, theirs, mine)], axis=1
        )

    def apply_t(p, v):
        a = stacked_parts(v)
        b = stacked_parts(turned(v))
        big = dot_nt(a, t_hi[p, 0]) + dot_nt(b, t_hi[p, 1])
        small = dot_nt(a[:ROWS], t_lo[p, 0]) + dot_nt(b[:ROWS], t_lo[p, 1])
        return big[:ROWS] + big[ROWS:] + small

    lax.fori_loop(0, SLOTS, find, 0)
    pair0.wait_recv()
    for p in range(2):
        fields[0][p] = apply_t(p, whole(incident[p], pair_e[0, p]))

    for it in range(ITERS):
        ns = [0]
        field = fields[it]

        def send_field(src, dst, recv_index, owner, it=it, ns=ns):
            k = ns[0]
            ns[0] += 1
            c = remote(src, dst, f_send.at[it, k], f_recv.at[it, recv_index], to_owner(owner))
            c.start()
            sends.append(c)

        def q0(kind, j):
            return kind * 4 + j

        def q1(kind, j):
            return 16 + j * 4 + kind

        def at(kind, j, row=None, field=field):
            k = (kind * 4 + j) * 2
            return field.at[pl.ds(k, 2)] if row is None else field.at[k + row]

        def arrive(ref, index, it=it):
            pltpu.make_async_copy(ref, ref, f_recv.at[it, index]).wait()

        own_z = {1: 0, 3: 1, 2: 2}
        near_g = {1: 3, 2: 4}

        halves = []
        for p in range(2):
            c = remote(
                field.at[p], pair_h.at[it, p], p_send.at[3 + it * 2 + p],
                p_recv.at[3 + it * 2 + p], other_core,
            )
            c.start()
            sends.append(c)
            halves.append(c)
        own = at(0, 0)
        send_field(own, at(0, 3), 1, along_z(1))
        send_field(own, at(0, 1), 0, along_z(3))
        send_field(own, at(2, 0), 4, along_g(1))
        send_field(own, at(1, 0), 3, along_g(-1))
        send_field(own, through_f.at[it], 5, along_y(y_way))

        for p in range(2):
            halves[p].wait_recv()
            v = whole(field[p], pair_h[it, p])
            wide[p, :, : 2 * HALF] = stacked_parts(v)
            wide[p, :, 2 * HALF :] = stacked_parts(turned(v))

        def load_block(n):
            fetch_block(n).wait()
            for c in range(2):
                hi, lo = split(stage[lax.rem(n, STAGES), c])
                m_hi[n, c * 512 : (c + 1) * 512] = hi
                m_lo[n, c * 512 : (c + 1) * 512] = lo

            @pl.when(n + STAGES < SLOTS)
            def _():
                fetch_block(n + STAGES).start()

        def backward(n, carry, it=it):
            if it == 0:
                load_block(n)
            left = wide[rows_ref[n]]
            big = dot_nn(left, m_hi[n])
            small = dot_nn(left[:ROWS], m_lo[n])
            result[n] = big[:ROWS] + big[ROWS:] + small
            return carry

        lax.fori_loop(0, 9, backward, 0)
        if it == 0:
            lax.fori_loop(1, 32, invert, 0)

        for j in (1, 3):
            arrive(at(0, j), own_z[j])
        send_field(
            field.at[pl.ds(jnp.where(even, 2, 6), 2)], at(0, 2), 2,
            jnp.where(even, along_z(3), along_z(1)),
        )
        for kind, dg in ((1, 1), (2, -1)):
            arrive(at(kind, 0), near_g[kind])
            send_field(at(kind, 0), transit.at[it, kind - 1], 6 + kind, along_g(-dg))
            send_field(at(kind, 0, 1), at(kind, 3, 1), 8 + kind, along_z(1))
            send_field(at(kind, 0, 1), at(kind, 1, 1), 10 + kind, along_z(3))
        for j in (1, 3):
            send_field(at(0, j, 0), at(2, j, 0), 12 + j, along_g(1))
            send_field(at(0, j, 0), at(1, j, 0), 16 + j, along_g(-1))
        arrive(through_f.at[it], 5)
        send_field(through_f.at[it], at(3, 0), 6, along_y(y_way))

        lax.fori_loop(9, 14, backward, 0)

        arrive(at(0, 2), 2)
        send_field(at(0, 2), at(2, 2), 14, along_g(1))
        send_field(at(0, 2), at(1, 2), 18, along_g(-1))
        arrive(transit.at[it, 0], 7)
        arrive(transit.at[it, 1], 8)
        send_field(transit.at[it, jnp.where(z < 3, 0, 1)], at(3, 3), 21, along_z(1))
        send_field(transit.at[it, jnp.where(z == 0, 0, 1)], at(3, 1), 16, along_z(3))

        lax.fori_loop(14, 18, backward, 0)

        arrive(at(3, 3), 21)
        arrive(at(3, 1), 16)
        send_field(
            field.at[pl.ds(jnp.where(even, 30, 26), 2)], at(3, 2), 20,
            jnp.where(even, along_z(1), along_z(3)),
        )

        lax.fori_loop(18, SLOTS, backward, 0)

        def fill(k, carry, it=it):
            flag = found[k].astype(F32)
            give[it, k] = result[slot_of[k]] * flag
            return carry

        lax.fori_loop(1, 32, fill, 0)

        ng = [0]

        def send_give(src, dst, recv_index, owner, it=it, ng=ng):
            k = ng[0]
            ng[0] += 1
            c = remote(src, dst, g_send.at[it, k], g_recv.at[it, recv_index], to_owner(owner))
            c.start()
            sends.append(c)

        def got_give(ref, index, it=it):
            pltpu.make_async_copy(ref, ref, g_recv.at[it, index]).wait()

        send_give(give.at[it, 4:8], from_x.at[it, 1], 1, along_g(1))
        send_give(give.at[it, 8:12], from_x.at[it, 0], 0, along_g(-1))
        for j in (1, 3, 2):
            send_give(give.at[it, pl.ds(16 + 4 * j, 4)], from_z.at[it, 4 - j], 6 + 4 - j, along_z(j))
        for j in (1, 2, 3):
            below = lax.rem(z + j, 4) < z
            send_give(
                give.at[it, q0(3, j)], from_x.at[it, 2, j], 2 + j,
                jnp.where(below, along_g(2), along_g(-2)),
            )
        send_give(give.at[it, q0(3, 0)], through_g.at[it, 0], 18, along_y(y_way))
        send_give(give.at[it, q1(3, 0)], through_g.at[it, 1], 19, along_y(y_way))

        for kind in (1, 2):
            arrive(at(kind, 3, 1), 8 + kind)
            arrive(at(kind, 1, 1), 10 + kind)
        for kind, base in ((2, 12), (1, 16)):
            for j in (1, 3):
                arrive(at(kind, j, 0), base + j)
            arrive(at(kind, 2), base + 2)
        arrive(at(3, 0), 6)
        arrive(at(3, 2), 20)

        for h in range(2):
            for p in range(2):
                near[it, h, p] = jnp.zeros((ROWS, HALF), F32)

        def forward(n, carry, it=it, field=field):
            v = field[place[n]]
            a = stacked_parts(v)
            b = stacked_parts(turned(v))
            big = dot_nt(a, m_hi[n, :512]) + dot_nt(b, m_hi[n, 512:])
            small = dot_nt(a[:ROWS], m_lo[n, :512]) + dot_nt(b[:ROWS], m_lo[n, 512:])
            out = big[:ROWS] + big[ROWS:] + small
            alive = (n < live_ref[0]).astype(F32)
            second = alive * rows_ref[n].astype(F32)
            first = alive - second
            for h in range(2):
                part = out[:, h * HALF : (h + 1) * HALF]
                near[it, h, 0] += part * first
                near[it, h, 1] += part * second
            return carry

        lax.fori_loop(0, SLOTS, forward, 0)

        c = remote(
            near.at[it, 1 - core], pair_n.at[it], p_send.at[7 + it], p_recv.at[7 + it], other_core
        )
        c.start()
        sends.append(c)

        got_give(through_g.at[it, 0], 18)
        send_give(through_g.at[it, 0], from_x.at[it, 2, 0], 2, along_y(y_way))
        got_give(through_g.at[it, 1], 19)
        send_give(through_g.at[it, 1], from_z.at[it, 0, 3], 6, along_y(y_way))
        for k in range(2):
            got_give(from_x.at[it, k], k)
        for j in range(1, 4):
            got_give(from_x.at[it, 2, j], 2 + j)
            line_sum[it, j] = (
                give[it, q0(0, j)] + from_x[it, 0, j] + from_x[it, 1, j] + from_x[it, 2, j]
            )
        for j in (1, 3, 2):
            send_give(line_sum.at[it, j], line_in.at[it, 4 - j], 10 + 4 - j, along_z(j))
        for j in range(1, 4):
            got_give(from_z.at[it, j], 6 + j)
        for k, kind in ((0, 1), (1, 2)):
            cross_sum[it, k] = (
                give[it, q1(kind, 0)]
                + from_z[it, 1, kind] + from_z[it, 2, kind] + from_z[it, 3, kind]
            )
        up = jnp.zeros((ROWS, HALF), F32)
        down = jnp.zeros((ROWS, HALF), F32)
        for j in range(1, 4):
            term = from_z[it, j, 3]
            above = (lax.rem(z + j, 4) > z).astype(F32)
            up += term * above
            down += term * (1.0 - above)
        cross_sum[it, 2] = up
        cross_sum[it, 3] = down
        for k, dg in ((0, 1), (1, -1), (2, 2), (3, -2)):
            send_give(cross_sum.at[it, k], cross_in.at[it, k], 14 + k, along_g(dg))

        got_give(from_x.at[it, 2, 0], 2)
        got_give(from_z.at[it, 0, 3], 6)
        for j in range(1, 4):
            got_give(line_in.at[it, j], 10 + j)
        for k in range(4):
            got_give(cross_in.at[it, k], 14 + k)
        c.wait_recv()
        returned0 = (
            from_x[it, 0, 0] + from_x[it, 1, 0] + from_x[it, 2, 0]
            + line_in[it, 1] + line_in[it, 2] + line_in[it, 3]
        )
        returned1 = (
            from_z[it, 1, 0] + from_z[it, 2, 0] + from_z[it, 3, 0] + from_z[it, 0, 3]
            + cross_in[it, 0] + cross_in[it, 1] + cross_in[it, 2] + cross_in[it, 3]
        )
        out_e[0] = incident[0] + near[it, core, 0] + pair_n[it, 0] + returned0
        out_e[1] = incident[1] + near[it, core, 1] + pair_n[it, 1] + returned1
        swap = remote(
            out_e, pair_e.at[1 + it], p_send.at[1 + it], p_recv.at[1 + it], other_core
        )
        swap.start()
        swap.wait()
        for p in range(2):
            after = apply_t(p, whole(out_e[p], pair_e[1 + it, p]))
            if it + 1 < ITERS:
                fields[it + 1][p] = after
            else:
                out_s[p] = after

    for c in sends:
        c.wait_send()


def settle(s_in, e_in, s_out, e_out):
    s_out[...] = s_in[...]
    e_out[...] = e_in[...]


def local(incident, tmat, blocks, block_rows, partners, live, owner_of):
    inc = incident.reshape(2, ROWS, HALF)
    vm = lambda shape, dt=F32: pltpu.VMEM(shape, dt)
    h = (ROWS, HALF)
    sem = pltpu.SemaphoreType.DMA
    shape = jax.ShapeDtypeStruct((2, ROWS, HALF), F32)
    scattered, exciting = pl.pallas_call(
        kernel,
        out_shape=(shape, shape),
        in_specs=[
            pl.BlockSpec(memory_space=pltpu.SMEM),
            pl.BlockSpec(memory_space=pltpu.SMEM),
            pl.BlockSpec(memory_space=pltpu.SMEM),
            pl.BlockSpec(memory_space=pltpu.SMEM),
            pl.BlockSpec(memory_space=pltpu.VMEM),
            pl.BlockSpec(memory_space=pl.ANY),
            pl.BlockSpec(memory_space=pl.ANY),
        ],
        out_specs=(pl.BlockSpec(memory_space=pltpu.VMEM),) * 2,
        scratch_shapes=[
            vm((32,) + h), vm((32,) + h), vm((2, 2, 2) + h), vm((2, 2) + h), vm((2, 2) + h), vm((2, 32) + h), vm((SLOTS,) + h),
            vm((2, 3, 4) + h), vm((2, 4) + h), vm((2, 4) + h), vm((2, 4, 4) + h),
            vm((2, 4) + h), vm((2, 4) + h),
            vm((3, 2) + h), vm((2, 2) + h), vm((2, 2) + h), vm((2, 2, 2) + h),
            vm((SLOTS, 1024, HALF), BF16), vm((SLOTS, 1024, HALF), BF16),
            vm((STAGES, 2, 512, HALF)),
            vm((2, 2, HALF, 512)), vm((2, 2, HALF, 512), BF16), vm((2, 2, HALF, 512), BF16),
            vm((2, 2 * ROWS, 1024), BF16),
            pltpu.SMEM((SLOTS,), jnp.int32), pltpu.SMEM((SLOTS,), jnp.int32),
            pltpu.SMEM((32,), jnp.int32), pltpu.SMEM((32,), jnp.int32),
            sem((2, 22)), sem((2, 22)), sem((2, 19)), sem((2, 20)), sem((9,)), sem((9,)),
            sem((STAGES,)), sem((1,)),
        ],
        compiler_params=pltpu.CompilerParams(
            collective_id=0, has_side_effects=True, vmem_limit_bytes=60 * 1024 * 1024
        ),
        name="scatter_steps",
    )(partners, owner_of, block_rows, live, inc, tmat, blocks)
    scattered, exciting = pl.pallas_call(settle, out_shape=(shape, shape), name="settle")(
        scattered, exciting
    )
    full = (2, 2, ROWS // 2, HALF)
    return scattered.reshape(full), exciting.reshape(full)


def solution(mesh):
    in_specs = (
        P("owner", None, None, "pair"),
        P("owner", None, "pair", None),
        P("owner", None, None, "pair"),
        P("owner"),
        P(),
        P("owner"),
        P(),
    )
    out_specs = (P("owner", None, None, "pair"), P("owner", None, None, "pair"))
    return jax.shard_map(local, mesh=mesh, in_specs=in_specs, out_specs=out_specs, check_vma=False)
```

time: 99.5 us -> 99.9 us (level)
  Pallas kernels: 91.8 us -> 98.5 us
  local copies, waits for them, and re-layouts: 5.16 us -> 0 us
    pallas_call x1, Pallas kernels: 91.8 us -> 96.8 us  [local(): pl.pallas_call(kernel, out_shape=(shape, shape), in_specs=[pl.BlockSpec(m...]
    unnamed x2 -> x0, local copies, waits for them, and re-layouts: 3.14 us -> none
    pallas_call x0 -> x1, Pallas kernels: none -> 1.68 us  [local(): pl.pallas_call(settle, out_shape=(shape, shape), name='settle')]
    concatenate x1 -> x0, local copies, waits for them, and re-layouts: 1.25 us -> none  [tables(): jnp.concatenate([where_, block_rows, alive, pad, slot_of, found])]
where the time goes in v2:
time: 99.9 us; the launch traced here: 99.8 us
  Pallas kernels  98.5 us (99%)
  between operations  1.29 us (1%)
    pallas_call x1, Pallas kernels, local(): pl.pallas_call(kernel, out_shape=(shape, shape), in_specs=[pl.BlockSpec(m...  96.8 us

profile of v2, /device:TPU:1, one launch (start us, length us, event | category | flops | bytes accessed | tf_op | source)
XLA Modules:
  0.0 99.8 jit_solution(5110622462011874422)
XLA Ops:
  1.3 96.8 %scatter_steps.1 = (f32[2,64,256]{2,1,0:T(8,128)}, f32[2,64,256]{2,1,0:T(8,128)}) custom-call(s32[1344]{0:T(1024)} %partners_ref.1, s32[128]{0:T(128)} %owner_ref.1, s32[21]{0:T(128)} %rows_ref.1, s32[1]{0:T(128)S(6)} %copy.9.live_ref, f32[2,64,256]{2,1,0:T(8,128)} %bitcast.3, f32[2,2,256,512]{3,2,1,0:T(8,128)} %tmat.1, f32[21,2,512,256]{3,2,1,0:T(8,128)} %blocks.1), custom_call_target="tpu_custom_call" | custom-call | tf_op jit(solution)/shard_map/scatter_steps/pallas_call | solution.py:409
  98.1 1.7 %settle.1 = (f32[2,64,256]{2,1,0:T(8,128)}, f32[2,64,256]{2,1,0:T(8,128)}) custom-call(f32[2,64,256]{2,1,0:T(8,128)} %get-tuple-element.6.s_in, f32[2,64,256]{2,1,0:T(8,128)} %get-tuple-element.7.e_in), custom_call_target="tpu_custom_call" | custom-call | tf_op jit(solution)/shard_map/settle/pallas_call | solution.py:441

commit v3 on v2

--- a/solution.py
+++ b/solution.py
@@ -90,9 +90,6 @@
 
     t_copy = pltpu.make_async_copy(tmat, t_raw, t_sem.at[0])
     t_copy.start()
-    for n in range(STAGES):
-        pltpu.make_async_copy(blocks.at[n], stage.at[n], stage_sem.at[n]).start()
-
     def find(n, carry):
         row = owner_ref[partners_ref[me * SLOTS + n]]
         owner = lax.div(row, 2)
@@ -100,8 +97,8 @@
         dg = lax.rem(lax.div(owner, 4) - group + 16, 16)
         kind = jnp.where(dg == 0, 0, jnp.where(dg == 1, 1, jnp.where(dg == 15, 2, 3)))
         which = lax.rem(row, 2)
-        place[n] = (kind * 4 + j) * 2 + which
         at = jnp.where(which == 0, kind * 4 + j, 16 + j * 4 + kind)
+        place[n] = at
         key[n] = jnp.where(n < live_ref[0], at, -1)
         return carry
 
@@ -117,6 +114,8 @@
         return carry
 
     t_copy.wait()
+    for n in range(STAGES):
+        pltpu.make_async_copy(blocks.at[n], stage.at[n], stage_sem.at[n]).start()
     for p in range(2):
         for c in range(2):
             hi, lo = split(t_raw[p, c])
@@ -145,56 +144,68 @@
         return big[:ROWS] + big[ROWS:] + small
 
     lax.fori_loop(0, SLOTS, find, 0)
+
+    def q0(kind, j):
+        return kind * 4 + j
+
+    def q1(kind, j):
+        return 16 + j * 4 + kind
+
+    counts = {}
+    halves = {}
+
+    def send_field(it, src, dst, recv_index, owner):
+        k = counts.get(it, 0)
+        counts[it] = k + 1
+        c = remote(src, dst, f_send.at[it, k], f_recv.at[it, recv_index], to_owner(owner))
+        c.start()
+        sends.append(c)
+
+    def share(it, p):
+        c = remote(
+            fields[it].at[16 * p], pair_h.at[it, p], p_send.at[5 + it * 2 + p],
+            p_recv.at[5 + it * 2 + p], other_core,
+        )
+        c.start()
+        sends.append(c)
+        halves[it, p] = c
+
+    def send_first(it):
+        f = fields[it]
+        for j in (2, 1, 3):
+            send_field(it, f.at[0], f.at[q0(0, 4 - j)], q0(0, 4 - j), along_z(j))
+        share(it, 0)
+
+    def send_second(it):
+        f = fields[it]
+        for dg, t in ((2, 1), (-2, 0)):
+            send_field(it, f.at[16], transit.at[it, t], 32 + t, along_g(dg))
+        for dg, kind in ((1, 2), (-1, 1)):
+            send_field(it, f.at[16], f.at[q1(kind, 0)], q1(kind, 0), along_g(dg))
+        share(it, 1)
+        send_field(it, f.at[0], through_f.at[it, 0], 34, along_y(y_way))
+        send_field(it, f.at[16], through_f.at[it, 1], 35, along_y(y_way))
+        for dg, kind in ((1, 2), (-1, 1)):
+            send_field(it, f.at[0], f.at[q0(kind, 0)], q0(kind, 0), along_g(dg))
+        for j in (2, 1, 3):
+            send_field(it, f.at[16], f.at[q1(0, 4 - j)], q1(0, 4 - j), along_z(j))
+
+    starts = (send_first, send_second)
     pair0.wait_recv()
     for p in range(2):
-        fields[0][p] = apply_t(p, whole(incident[p], pair_e[0, p]))
+        fields[0][16 * p] = apply_t(p, whole(incident[p], pair_e[0, p]))
+        starts[p](0)
 
     for it in range(ITERS):
-        ns = [0]
         field = fields[it]
 
-        def send_field(src, dst, recv_index, owner, it=it, ns=ns):
-            k = ns[0]
-            ns[0] += 1
-            c = remote(src, dst, f_send.at[it, k], f_recv.at[it, recv_index], to_owner(owner))
-            c.start()
-            sends.append(c)
-
-        def q0(kind, j):
-            return kind * 4 + j
-
-        def q1(kind, j):
-            return 16 + j * 4 + kind
-
-        def at(kind, j, row=None, field=field):
-            k = (kind * 4 + j) * 2
-            return field.at[pl.ds(k, 2)] if row is None else field.at[k + row]
-
-        def arrive(ref, index, it=it):
+        def got_field(index, it=it, field=field):
+            ref = field.at[index] if index < 32 else transit.at[it, index - 32]
             pltpu.make_async_copy(ref, ref, f_recv.at[it, index]).wait()
 
-        own_z = {1: 0, 3: 1, 2: 2}
-        near_g = {1: 3, 2: 4}
-
-        halves = []
         for p in range(2):
-            c = remote(
-                field.at[p], pair_h.at[it, p], p_send.at[3 + it * 2 + p],
-                p_recv.at[3 + it * 2 + p], other_core,
-            )
-            c.start()
-            sends.append(c)
-            halves.append(c)
-        own = at(0, 0)
-        send_field(own, at(0, 3), 1, along_z(1))
-        send_field(own, at(0, 1), 0, along_z(3))
-        send_field(own, at(2, 0), 4, along_g(1))
-        send_field(own, at(1, 0), 3, along_g(-1))
-        send_field(own, through_f.at[it], 5, along_y(y_way))
-
-        for p in range(2):
-            halves[p].wait_recv()
-            v = whole(field[p], pair_h[it, p])
+            halves[it, p].wait_recv()
+            v = whole(field[16 * p], pair_h[it, p])
             wide[p, :, : 2 * HALF] = stacked_parts(v)
             wide[p, :, 2 * HALF :] = stacked_parts(turned(v))
 
@@ -218,47 +229,43 @@
             result[n] = big[:ROWS] + big[ROWS:] + small
             return carry
 
-        lax.fori_loop(0, 9, backward, 0)
+        lax.fori_loop(0, 10, backward, 0)
         if it == 0:
             lax.fori_loop(1, 32, invert, 0)
 
-        for j in (1, 3):
-            arrive(at(0, j), own_z[j])
-        send_field(
-            field.at[pl.ds(jnp.where(even, 2, 6), 2)], at(0, 2), 2,
-            jnp.where(even, along_z(3), along_z(1)),
-        )
-        for kind, dg in ((1, 1), (2, -1)):
-            arrive(at(kind, 0), near_g[kind])
-            send_field(at(kind, 0), transit.at[it, kind - 1], 6 + kind, along_g(-dg))
-            send_field(at(kind, 0, 1), at(kind, 3, 1), 8 + kind, along_z(1))
-            send_field(at(kind, 0, 1), at(kind, 1, 1), 10 + kind, along_z(3))
-        for j in (1, 3):
-            send_field(at(0, j, 0), at(2, j, 0), 12 + j, along_g(1))
-            send_field(at(0, j, 0), at(1, j, 0), 16 + j, along_g(-1))
-        arrive(through_f.at[it], 5)
-        send_field(through_f.at[it], at(3, 0), 6, along_y(y_way))
-
-        lax.fori_loop(9, 14, backward, 0)
-
-        arrive(at(0, 2), 2)
-        send_field(at(0, 2), at(2, 2), 14, along_g(1))
-        send_field(at(0, 2), at(1, 2), 18, along_g(-1))
-        arrive(transit.at[it, 0], 7)
-        arrive(transit.at[it, 1], 8)
-        send_field(transit.at[it, jnp.where(z < 3, 0, 1)], at(3, 3), 21, along_z(1))
-        send_field(transit.at[it, jnp.where(z == 0, 0, 1)], at(3, 1), 16, along_z(3))
-
-        lax.fori_loop(14, 18, backward, 0)
-
-        arrive(at(3, 3), 21)
-        arrive(at(3, 1), 16)
-        send_field(
-            field.at[pl.ds(jnp.where(even, 30, 26), 2)], at(3, 2), 20,
-            jnp.where(even, along_z(1), along_z(3)),
-        )
-
-        lax.fori_loop(18, SLOTS, backward, 0)
+        got_field(32)
+        got_field(33)
+        for j in (2, 1, 3):
+            above = lax.rem(z + j, 4) > z
+            send_field(
+                it, transit.at[it, jnp.where(above, 0, 1)], field.at[q1(3, 4 - j)],
+                q1(3, 4 - j), along_z(j),
+            )
+        for j in (1, 3, 2):
+            got_field(q0(0, j))
+            line = field.at[q0(0, j)]
+            above = lax.rem(z + j, 4) > z
+            send_field(
+                it, line, field.at[q0(3, j)], q0(3, j),
+                jnp.where(above, along_g(2), along_g(-2)),
+            )
+            for dg, kind in ((1, 2), (-1, 1)):
+                send_field(it, line, field.at[q0(kind, j)], q0(kind, j), along_g(dg))
+        for kind in (1, 2):
+            got_field(q1(kind, 0))
+            for j in (2, 1, 3):
+                send_field(
+                    it, field.at[q1(kind, 0)], field.at[q1(kind, 4 - j)],
+                    q1(kind, 4 - j), along_z(j),
+                )
+        for p in range(2):
+            pltpu.make_async_copy(
+                through_f.at[it, p], through_f.at[it, p], f_recv.at[it, 34 + p]
+            ).wait()
+            there = (q0(3, 0), q1(3, 0))[p]
+            send_field(it, through_f.at[it, p], field.at[there], there, along_y(y_way))
+
+        lax.fori_loop(10, SLOTS, backward, 0)
 
         def fill(k, carry, it=it):
             flag = found[k].astype(F32)
@@ -279,28 +286,34 @@
         def got_give(ref, index, it=it):
             pltpu.make_async_copy(ref, ref, g_recv.at[it, index]).wait()
 
-        send_give(give.at[it, 4:8], from_x.at[it, 1], 1, along_g(1))
-        send_give(give.at[it, 8:12], from_x.at[it, 0], 0, along_g(-1))
-        for j in (1, 3, 2):
-            send_give(give.at[it, pl.ds(16 + 4 * j, 4)], from_z.at[it, 4 - j], 6 + 4 - j, along_z(j))
+        for j in (2, 1, 3):
+            send_give(
+                give.at[it, pl.ds(17 + 4 * j, 3)], from_z.at[it, 4 - j, pl.ds(1, 3)], 6 + 4 - j,
+                along_z(j),
+            )
         for j in (1, 2, 3):
             below = lax.rem(z + j, 4) < z
             send_give(
                 give.at[it, q0(3, j)], from_x.at[it, 2, j], 2 + j,
                 jnp.where(below, along_g(2), along_g(-2)),
             )
+        send_give(give.at[it, 5:8], from_x.at[it, 1, pl.ds(1, 3)], 1, along_g(1))
+        send_give(give.at[it, 9:12], from_x.at[it, 0, pl.ds(1, 3)], 0, along_g(-1))
         send_give(give.at[it, q0(3, 0)], through_g.at[it, 0], 18, along_y(y_way))
         send_give(give.at[it, q1(3, 0)], through_g.at[it, 1], 19, along_y(y_way))
-
-        for kind in (1, 2):
-            arrive(at(kind, 3, 1), 8 + kind)
-            arrive(at(kind, 1, 1), 10 + kind)
-        for kind, base in ((2, 12), (1, 16)):
-            for j in (1, 3):
-                arrive(at(kind, j, 0), base + j)
-            arrive(at(kind, 2), base + 2)
-        arrive(at(3, 0), 6)
-        arrive(at(3, 2), 20)
+        for j in (1, 3, 2):
+            send_give(give.at[it, 16 + 4 * j], from_z.at[it, 4 - j, 0], 19 + 4 - j, along_z(j))
+        send_give(give.at[it, 4], from_x.at[it, 1, 0], 24, along_g(1))
+        send_give(give.at[it, 8], from_x.at[it, 0, 0], 23, along_g(-1))
+
+        for kind in range(4):
+            for j in range(4):
+                if kind == 0 and j == 0:
+                    continue
+                if not (kind == 0):
+                    got_field(q0(kind, j))
+                if not (j == 0 and kind in (1, 2)):
+                    got_field(q1(kind, j))
 
         for h in range(2):
             for p in range(2):
@@ -322,20 +335,14 @@
                 near[it, h, 1] += part * second
             return carry
 
-        lax.fori_loop(0, SLOTS, forward, 0)
-
-        c = remote(
-            near.at[it, 1 - core], pair_n.at[it], p_send.at[7 + it], p_recv.at[7 + it], other_core
-        )
-        c.start()
-        sends.append(c)
+        lax.fori_loop(0, 14, forward, 0)
 
         got_give(through_g.at[it, 0], 18)
         send_give(through_g.at[it, 0], from_x.at[it, 2, 0], 2, along_y(y_way))
         got_give(through_g.at[it, 1], 19)
         send_give(through_g.at[it, 1], from_z.at[it, 0, 3], 6, along_y(y_way))
         for k in range(2):
-            got_give(from_x.at[it, k], k)
+            got_give(from_x.at[it, k, pl.ds(1, 3)], k)
         for j in range(1, 4):
             got_give(from_x.at[it, 2, j], 2 + j)
             line_sum[it, j] = (
@@ -344,7 +351,7 @@
         for j in (1, 3, 2):
             send_give(line_sum.at[it, j], line_in.at[it, 4 - j], 10 + 4 - j, along_z(j))
         for j in range(1, 4):
-            got_give(from_z.at[it, j], 6 + j)
+            got_give(from_z.at[it, j, pl.ds(1, 3)], 6 + j)
         for k, kind in ((0, 1), (1, 2)):
             cross_sum[it, k] = (
                 give[it, q1(kind, 0)]
@@ -362,32 +369,50 @@
         for k, dg in ((0, 1), (1, -1), (2, 2), (3, -2)):
             send_give(cross_sum.at[it, k], cross_in.at[it, k], 14 + k, along_g(dg))
 
-        got_give(from_x.at[it, 2, 0], 2)
-        got_give(from_z.at[it, 0, 3], 6)
-        for j in range(1, 4):
-            got_give(line_in.at[it, j], 10 + j)
-        for k in range(4):
-            got_give(cross_in.at[it, k], 14 + k)
+        lax.fori_loop(14, SLOTS, forward, 0)
+
+        c = remote(
+            near.at[it, 1 - core], pair_n.at[it], p_send.at[9 + it], p_recv.at[9 + it], other_core
+        )
+        c.start()
+        sends.append(c)
+
         c.wait_recv()
-        returned0 = (
-            from_x[it, 0, 0] + from_x[it, 1, 0] + from_x[it, 2, 0]
-            + line_in[it, 1] + line_in[it, 2] + line_in[it, 3]
-        )
-        returned1 = (
-            from_z[it, 1, 0] + from_z[it, 2, 0] + from_z[it, 3, 0] + from_z[it, 0, 3]
-            + cross_in[it, 0] + cross_in[it, 1] + cross_in[it, 2] + cross_in[it, 3]
-        )
-        out_e[0] = incident[0] + near[it, core, 0] + pair_n[it, 0] + returned0
-        out_e[1] = incident[1] + near[it, core, 1] + pair_n[it, 1] + returned1
-        swap = remote(
-            out_e, pair_e.at[1 + it], p_send.at[1 + it], p_recv.at[1 + it], other_core
-        )
-        swap.start()
-        swap.wait()
+        swaps = []
         for p in range(2):
+            if p == 0:
+                got_give(from_x.at[it, 2, 0], 2)
+                for k in range(2):
+                    got_give(from_x.at[it, k, 0], 23 + k)
+                for j in range(1, 4):
+                    got_give(line_in.at[it, j], 10 + j)
+                returned = (
+                    from_x[it, 0, 0] + from_x[it, 1, 0] + from_x[it, 2, 0]
+                    + line_in[it, 1] + line_in[it, 2] + line_in[it, 3]
+                )
+            else:
+                got_give(from_z.at[it, 0, 3], 6)
+                for j in range(1, 4):
+                    got_give(from_z.at[it, j, 0], 19 + j)
+                for k in range(4):
+                    got_give(cross_in.at[it, k], 14 + k)
+                returned = (
+                    from_z[it, 1, 0] + from_z[it, 2, 0] + from_z[it, 3, 0] + from_z[it, 0, 3]
+                    + cross_in[it, 0] + cross_in[it, 1] + cross_in[it, 2] + cross_in[it, 3]
+                )
+            out_e[p] = incident[p] + near[it, core, p] + pair_n[it, p] + returned
+            swap = remote(
+                out_e.at[p], pair_e.at[1 + it, p], p_send.at[1 + 2 * it + p],
+                p_recv.at[1 + 2 * it + p], other_core,
+            )
+            swap.start()
+            swaps.append(swap)
+        for p in range(2):
+            swaps[p].wait()
             after = apply_t(p, whole(out_e[p], pair_e[1 + it, p]))
             if it + 1 < ITERS:
-                fields[it + 1][p] = after
+                fields[it + 1][16 * p] = after
+                starts[p](it + 1)
             else:
                 out_s[p] = after
 
@@ -420,7 +445,7 @@
         ],
         out_specs=(pl.BlockSpec(memory_space=pltpu.VMEM),) * 2,
         scratch_shapes=[
-            vm((32,) + h), vm((32,) + h), vm((2, 2, 2) + h), vm((2, 2) + h), vm((2, 2) + h), vm((2, 32) + h), vm((SLOTS,) + h),
+            vm((32,) + h), vm((32,) + h), vm((2, 2) + h), vm((2, 2) + h), vm((2, 2) + h), vm((2, 32) + h), vm((SLOTS,) + h),
             vm((2, 3, 4) + h), vm((2, 4) + h), vm((2, 4) + h), vm((2, 4, 4) + h),
             vm((2, 4) + h), vm((2, 4) + h),
             vm((3, 2) + h), vm((2, 2) + h), vm((2, 2) + h), vm((2, 2, 2) + h),
@@ -430,7 +455,7 @@
             vm((2, 2 * ROWS, 1024), BF16),
             pltpu.SMEM((SLOTS,), jnp.int32), pltpu.SMEM((SLOTS,), jnp.int32),
             pltpu.SMEM((32,), jnp.int32), pltpu.SMEM((32,), jnp.int32),
-            sem((2, 22)), sem((2, 22)), sem((2, 19)), sem((2, 20)), sem((9,)), sem((9,)),
+            sem((2, 34)), sem((2, 36)), sem((2, 24)), sem((2, 25)), sem((11,)), sem((11,)),
             sem((STAGES,)), sem((1,)),
         ],
         compiler_params=pltpu.CompilerParams(

time: 99.9 us -> 90.6 us (0.907)
  Pallas kernels: 98.5 us -> 89 us
    pallas_call x1, Pallas kernels: 96.8 us -> 87.4 us  [local(): pl.pallas_call(kernel, out_shape=(shape, shape), in_specs=[pl.BlockSpec(m...]
where the time goes in v3:
time: 90.6 us; the launch traced here: 90.3 us
  Pallas kernels  89 us (98%)
  between operations  1.29 us (1%)
    pallas_call x1, Pallas kernels, local(): pl.pallas_call(kernel, out_shape=(shape, shape), in_specs=[pl.BlockSpec(m...  87.4 us

profile of v3, /device:TPU:1, one launch (start us, length us, event | category | flops | bytes accessed | tf_op | source)
XLA Modules:
  0.0 90.3 jit_solution(1526626543753556217)
XLA Ops:
  1.3 87.4 %scatter_steps.1 = (f32[2,64,256]{2,1,0:T(8,128)}, f32[2,64,256]{2,1,0:T(8,128)}) custom-call(s32[1344]{0:T(1024)} %partners_ref.1, s32[128]{0:T(128)} %owner_ref.1, s32[21]{0:T(128)} %rows_ref.1, s32[1]{0:T(128)S(6)} %copy.9.live_ref, f32[2,64,256]{2,1,0:T(8,128)} %bitcast.3, f32[2,2,256,512]{3,2,1,0:T(8,128)} %tmat.1, f32[21,2,512,256]{3,2,1,0:T(8,128)} %blocks.1), custom_call_target="tpu_custom_call" | custom-call | tf_op jit(solution)/shard_map/scatter_steps/pallas_call | solution.py:434
  88.7 1.7 %settle.1 = (f32[2,64,256]{2,1,0:T(8,128)}, f32[2,64,256]{2,1,0:T(8,128)}) custom-call(f32[2,64,256]{2,1,0:T(8,128)} %get-tuple-element.6.s_in, f32[2,64,256]{2,1,0:T(8,128)} %get-tuple-element.7.e_in), custom_call_target="tpu_custom_call" | custom-call | tf_op jit(solution)/shard_map/settle/pallas_call | solution.py:466

commit v4 on v3

--- a/solution.py
+++ b/solution.py
@@ -172,16 +172,16 @@
 
     def send_first(it):
         f = fields[it]
-        for j in (2, 1, 3):
+        for j in (1, 3, 2):
             send_field(it, f.at[0], f.at[q0(0, 4 - j)], q0(0, 4 - j), along_z(j))
         share(it, 0)
 
     def send_second(it):
         f = fields[it]
+        for dg, kind in ((1, 2), (-1, 1)):
+            send_field(it, f.at[16], f.at[q1(kind, 0)], q1(kind, 0), along_g(dg))
         for dg, t in ((2, 1), (-2, 0)):
             send_field(it, f.at[16], transit.at[it, t], 32 + t, along_g(dg))
-        for dg, kind in ((1, 2), (-1, 1)):
-            send_field(it, f.at[16], f.at[q1(kind, 0)], q1(kind, 0), along_g(dg))
         share(it, 1)
         send_field(it, f.at[0], through_f.at[it, 0], 34, along_y(y_way))
         send_field(it, f.at[16], through_f.at[it, 1], 35, along_y(y_way))
@@ -229,9 +229,38 @@
             result[n] = big[:ROWS] + big[ROWS:] + small
             return carry
 
-        lax.fori_loop(0, 10, backward, 0)
+        def forward_line(j, it=it, field=field):
+            line = field.at[q0(0, j)]
+            for dg, kind in ((1, 2), (-1, 1)):
+                send_field(it, line, field.at[q0(kind, j)], q0(kind, j), along_g(dg))
+            above = lax.rem(z + j, 4) > z
+            send_field(
+                it, line, field.at[q0(3, j)], q0(3, j),
+                jnp.where(above, along_g(2), along_g(-2)),
+            )
+
+        lax.fori_loop(0, 8, backward, 0)
+
+        for j in (1, 3):
+            got_field(q0(0, j))
+            forward_line(j)
+        for kind in (1, 2):
+            got_field(q1(kind, 0))
+            for j in (2, 1, 3):
+                send_field(
+                    it, field.at[q1(kind, 0)], field.at[q1(kind, 4 - j)], q1(kind, 4 - j),
+                    along_z(j),
+                )
+        for p in range(2):
+            pltpu.make_async_copy(
+                through_f.at[it, p], through_f.at[it, p], f_recv.at[it, 34 + p]
+            ).wait()
+            there = (q0(3, 0), q1(3, 0))[p]
+            send_field(it, through_f.at[it, p], field.at[there], there, along_y(y_way))
         if it == 0:
             lax.fori_loop(1, 32, invert, 0)
+
+        lax.fori_loop(8, 13, backward, 0)
 
         got_field(32)
         got_field(33)
@@ -241,31 +270,10 @@
                 it, transit.at[it, jnp.where(above, 0, 1)], field.at[q1(3, 4 - j)],
                 q1(3, 4 - j), along_z(j),
             )
-        for j in (1, 3, 2):
-            got_field(q0(0, j))
-            line = field.at[q0(0, j)]
-            above = lax.rem(z + j, 4) > z
-            send_field(
-                it, line, field.at[q0(3, j)], q0(3, j),
-                jnp.where(above, along_g(2), along_g(-2)),
-            )
-            for dg, kind in ((1, 2), (-1, 1)):
-                send_field(it, line, field.at[q0(kind, j)], q0(kind, j), along_g(dg))
-        for kind in (1, 2):
-            got_field(q1(kind, 0))
-            for j in (2, 1, 3):
-                send_field(
-                    it, field.at[q1(kind, 0)], field.at[q1(kind, 4 - j)],
-                    q1(kind, 4 - j), along_z(j),
-                )
-        for p in range(2):
-            pltpu.make_async_copy(
-                through_f.at[it, p], through_f.at[it, p], f_recv.at[it, 34 + p]
-            ).wait()
-            there = (q0(3, 0), q1(3, 0))[p]
-            send_field(it, through_f.at[it, p], field.at[there], there, along_y(y_way))
-
-        lax.fori_loop(10, SLOTS, backward, 0)
+        got_field(q0(0, 2))
+        forward_line(2)
+
+        lax.fori_loop(13, SLOTS, backward, 0)
 
         def fill(k, carry, it=it):
             flag = found[k].astype(F32)
@@ -335,12 +343,12 @@
                 near[it, h, 1] += part * second
             return carry
 
-        lax.fori_loop(0, 14, forward, 0)
-
         got_give(through_g.at[it, 0], 18)
         send_give(through_g.at[it, 0], from_x.at[it, 2, 0], 2, along_y(y_way))
         got_give(through_g.at[it, 1], 19)
         send_give(through_g.at[it, 1], from_z.at[it, 0, 3], 6, along_y(y_way))
+        lax.fori_loop(0, 10, forward, 0)
+
         for k in range(2):
             got_give(from_x.at[it, k, pl.ds(1, 3)], k)
         for j in range(1, 4):
@@ -369,7 +377,7 @@
         for k, dg in ((0, 1), (1, -1), (2, 2), (3, -2)):
             send_give(cross_sum.at[it, k], cross_in.at[it, k], 14 + k, along_g(dg))
 
-        lax.fori_loop(14, SLOTS, forward, 0)
+        lax.fori_loop(10, SLOTS, forward, 0)
 
         c = remote(
             near.at[it, 1 - core], pair_n.at[it], p_send.at[9 + it], p_recv.at[9 + it], other_core

time: 90.6 us -> 88.8 us (0.980)
  Pallas kernels: 89 us -> 87.3 us
    pallas_call x1, Pallas kernels: 87.4 us -> 85.7 us  [local(): pl.pallas_call(kernel, out_shape=(shape, shape), in_specs=[pl.BlockSpec(m...]
where the time goes in v4:
time: 88.8 us; the launch traced here: 88.6 us
  Pallas kernels  87.3 us (98%)
  between operations  1.29 us (1%)
    pallas_call x1, Pallas kernels, local(): pl.pallas_call(kernel, out_shape=(shape, shape), in_specs=[pl.BlockSpec(m...  85.7 us

profile of v4, /device:TPU:1, one launch (start us, length us, event | category | flops | bytes accessed | tf_op | source)
XLA Modules:
  0.0 88.6 jit_solution(15910400879081160392)
XLA Ops:
  1.3 85.7 %scatter_steps.1 = (f32[2,64,256]{2,1,0:T(8,128)}, f32[2,64,256]{2,1,0:T(8,128)}) custom-call(s32[1344]{0:T(1024)} %partners_ref.1, s32[128]{0:T(128)} %owner_ref.1, s32[21]{0:T(128)} %rows_ref.1, s32[1]{0:T(128)S(6)} %copy.9.live_ref, f32[2,64,256]{2,1,0:T(8,128)} %bitcast.3, f32[2,2,256,512]{3,2,1,0:T(8,128)} %tmat.1, f32[21,2,512,256]{3,2,1,0:T(8,128)} %blocks.1), custom_call_target="tpu_custom_call" | custom-call | tf_op jit(solution)/shard_map/scatter_steps/pallas_call | solution.py:442
  86.9 1.7 %settle.1 = (f32[2,64,256]{2,1,0:T(8,128)}, f32[2,64,256]{2,1,0:T(8,128)}) custom-call(f32[2,64,256]{2,1,0:T(8,128)} %get-tuple-element.6.s_in, f32[2,64,256]{2,1,0:T(8,128)} %get-tuple-element.7.e_in), custom_call_target="tpu_custom_call" | custom-call | tf_op jit(solution)/shard_map/settle/pallas_call | solution.py:474

commit v5 on v4

--- a/solution.py
+++ b/solution.py
@@ -239,7 +239,7 @@
                 jnp.where(above, along_g(2), along_g(-2)),
             )
 
-        lax.fori_loop(0, 8, backward, 0)
+        lax.fori_loop(0, 7, backward, 0)
 
         for j in (1, 3):
             got_field(q0(0, j))
@@ -260,7 +260,7 @@
         if it == 0:
             lax.fori_loop(1, 32, invert, 0)
 
-        lax.fori_loop(8, 13, backward, 0)
+        lax.fori_loop(7, 11, backward, 0)
 
         got_field(32)
         got_field(33)
@@ -273,7 +273,7 @@
         got_field(q0(0, 2))
         forward_line(2)
 
-        lax.fori_loop(13, SLOTS, backward, 0)
+        lax.fori_loop(11, SLOTS, backward, 0)
 
         def fill(k, carry, it=it):
             flag = found[k].astype(F32)
@@ -347,7 +347,7 @@
         send_give(through_g.at[it, 0], from_x.at[it, 2, 0], 2, along_y(y_way))
         got_give(through_g.at[it, 1], 19)
         send_give(through_g.at[it, 1], from_z.at[it, 0, 3], 6, along_y(y_way))
-        lax.fori_loop(0, 10, forward, 0)
+        lax.fori_loop(0, 9, forward, 0)
 
         for k in range(2):
             got_give(from_x.at[it, k, pl.ds(1, 3)], k)
@@ -377,7 +377,7 @@
         for k, dg in ((0, 1), (1, -1), (2, 2), (3, -2)):
             send_give(cross_sum.at[it, k], cross_in.at[it, k], 14 + k, along_g(dg))
 
-        lax.fori_loop(10, SLOTS, forward, 0)
+        lax.fori_loop(9, SLOTS, forward, 0)
 
         c = remote(
             near.at[it, 1 - core], pair_n.at[it], p_send.at[9 + it], p_recv.at[9 + it], other_core

time: 88.8 us -> 89.6 us (level)
  no operation moved by 1% of the time
where the time goes in v5:
time: 89.6 us; the launch traced here: 89.3 us
  Pallas kernels  88.1 us (98%)
  between operations  1.29 us (1%)
    pallas_call x1, Pallas kernels, local(): pl.pallas_call(kernel, out_shape=(shape, shape), in_specs=[pl.BlockSpec(m...  86.4 us

profile of v5, /device:TPU:1, one launch (start us, length us, event | category | flops | bytes accessed | tf_op | source)
XLA Modules:
  0.0 89.3 jit_solution(2482288181897938719)
XLA Ops:
  1.3 86.4 %scatter_steps.1 = (f32[2,64,256]{2,1,0:T(8,128)}, f32[2,64,256]{2,1,0:T(8,128)}) custom-call(s32[1344]{0:T(1024)} %partners_ref.1, s32[128]{0:T(128)} %owner_ref.1, s32[21]{0:T(128)} %rows_ref.1, s32[1]{0:T(128)S(6)} %copy.9.live_ref, f32[2,64,256]{2,1,0:T(8,128)} %bitcast.3, f32[2,2,256,512]{3,2,1,0:T(8,128)} %tmat.1, f32[21,2,512,256]{3,2,1,0:T(8,128)} %blocks.1), custom_call_target="tpu_custom_call" | custom-call | tf_op jit(solution)/shard_map/scatter_steps/pallas_call | solution.py:442
  87.7 1.7 %settle.1 = (f32[2,64,256]{2,1,0:T(8,128)}, f32[2,64,256]{2,1,0:T(8,128)}) custom-call(f32[2,64,256]{2,1,0:T(8,128)} %get-tuple-element.6.s_in, f32[2,64,256]{2,1,0:T(8,128)} %get-tuple-element.7.e_in), custom_call_target="tpu_custom_call" | custom-call | tf_op jit(solution)/shard_map/settle/pallas_call | solution.py:474
